TPU v7x, 32 devices: a whole 2x2x4 slice. The times are simulated.
32 devices in a mesh: rep: 2 (over x), ctx: 8 (over z, y), tp: 2 (over core).
Axes of the slice: x: 2, y: 2, z: 4, core: 2. Of those that a mesh axis runs over, the one named last changes fastest.
Arguments:
- queries: bfloat16 [4096, 4096], P(('rep', 'ctx'), 'tp'), parts along dimension 0, may hold values from -8 to 8
- rotated_key_rows: bfloat16 [4096, 512], P(('rep', 'ctx'), 'tp'), parts along dimension 0, may hold values from -8 to 8
- ordered_value_rows: bfloat16 [4096, 512], P(('rep', 'ctx'), 'tp'), parts along dimension 0, may hold values from -6 to 6
- block_order: int32 [32], P('rep'), parts along dimension 0, may hold values from 0 to 15, each once
- live_blocks: int32 [32, 12], P('rep'), parts along dimension 0, may hold values from -1 to 15, as said below
Outputs:
- attended: bfloat16 [4096, 4096], P(('rep', 'ctx', 'tp')), parts along dimension 0
- log_norm: float32 [64, 2048], P(('rep', 'tp'), 'ctx'), parts along dimension 0
There are 2 independent parts, one for each index of `rep`. A program takes and returns all parts, laid end to end along the dimension named above; each array names one. Nothing has to cross between parts.
Inputs may be any that keep to these rules, and one draw needn't show every extreme that they name: `live_blocks`: row s names block s in its first slot, then distinct blocks before s, then -1 in every unused slot; row 15 fills all 12 slots.
All inputs are finite; a program needn't handle non-finite values.
Results may differ from a plain program's by a relative error of at most 0.008.
Values may be sent and summed in bfloat16 or wider, within the bound.
A program may use at most 128 MiB of HBM per device.

v0:
```python
import functools
import math

import jax
import jax.numpy as jnp
from jax import lax
from jax.experimental import pallas as pl
from jax.experimental.pallas import tpu as pltpu
from jax.sharding import PartitionSpec as P

HEAD_SIZE = 128
BLOCK_TOKENS = 128
CHUNK = 256
FAR = 1e30
HUGE = 3e38
MESH = pl.DeviceIdType.MESH


def grid_of(count):
    minor = max(d for d in range(1, math.isqrt(count) + 1) if count % d == 0)
    return count // minor, minor


def kernel(
    dims,
    queries,
    keys,
    values,
    block_order,
    live_blocks,
    attended,
    log_norm,
    held,
    raw_queries,
    turned_queries,
    total,
    peak,
    weight_sum,
    leaving,
    limits,
    load_sem,
    send_sem,
    recv_sem,
    swap_send,
    swap_recv,
):
    major, minor, tp_size, kv_local, groups, blocks_here, slots_live = dims
    factor = HEAD_SIZE ** (-0.5)
    scale = factor * math.log2(math.e)
    width = groups * BLOCK_TOKENS
    rows = blocks_here * BLOCK_TOKENS
    me = lax.axis_index("ctx")
    mine = lax.axis_index("tp")
    a, b = me // minor, me % minor

    loads = [
        pltpu.make_async_copy(keys, held.at[me, 0], load_sem.at[0]),
        pltpu.make_async_copy(values, held.at[me, 1], load_sem.at[1]),
        pltpu.make_async_copy(queries, raw_queries, load_sem.at[2]),
    ]
    for load in loads:
        load.start()

    barrier = pltpu.get_barrier_semaphore()
    sides = (
        (a > 0, me - minor),
        (a < major - 1, me + minor),
        (b > 0, me - 1),
        (b < minor - 1, me + 1),
    )
    for there, who in sides:

        @pl.when(there)
        def _(who=who):
            pl.semaphore_signal(barrier, inc=1, device_id={"ctx": who}, device_id_type=MESH)

    for turn in range(1, tp_size):
        peer = (mine + turn) % tp_size
        pl.semaphore_signal(barrier, inc=1, device_id={"tp": peer}, device_id_type=MESH)
    expected = jnp.int32(tp_size - 1)
    for there, _ in sides:
        expected = expected + there.astype(jnp.int32)
    pl.semaphore_wait(barrier, expected)

    def onward(slot, piece, i, j):
        wanted = (
            (j == b) & (i >= a) & (a > 0),
            (j == b) & (i <= a) & (a < major - 1),
            (j >= b) & (b > 0),
            (j <= b) & (b < minor - 1),
        )
        for side in range(4):
            copy = pltpu.make_async_remote_copy(
                src_ref=held.at[slot, piece],
                dst_ref=held.at[slot, piece],
                send_sem=send_sem.at[slot, piece, side],
                recv_sem=recv_sem.at[slot, piece],
                device_id={"ctx": sides[side][1]},
                device_id_type=MESH,
            )
            yield wanted[side], copy

    def send_on(slot, piece, i, j):
        for wanted, copy in onward(slot, piece, i, j):

            @pl.when(wanted)
            def _(copy=copy):
                copy.start()

    def find_limits(slot):
        for query_block in range(blocks_here):
            my_seq = block_order[0, me * blocks_here + query_block]
            found = [jnp.bool_(False)] * blocks_here
            names = [block_order[0, slot * blocks_here + kb] for kb in range(blocks_here)]
            for entry in range(slots_live):
                listed = live_blocks[my_seq, entry]
                found = [f | (listed == name) for f, name in zip(found, names)]
            for kb in range(blocks_here):
                limits[0, query_block * blocks_here + kb] = jnp.where(found[kb], HUGE, -FAR)
                limits[1, query_block * blocks_here + kb] = jnp.where(found[kb], -HUGE, FAR)

    def attend(slot, own):
        find_limits(slot)
        for h in range(kv_local):
            columns = pl.ds(h * HEAD_SIZE, HEAD_SIZE)
            key_part = held[slot, 0, :, columns]
            value_part = jnp.transpose(held[slot, 1, :, columns])

            def one_query_block(query_block, carry):
                caps = [limits[0, query_block * blocks_here + kb] for kb in range(blocks_here)]
                floors = [limits[1, query_block * blocks_here + kb] for kb in range(blocks_here)]
                for start in range(0, width, CHUNK):
                    lanes = pl.ds(start, CHUNK)
                    scores = jnp.dot(
                        key_part,
                        turned_queries[query_block, h, :, lanes],
                        preferred_element_type=jnp.float32,
                    )
                    parts = []
                    for kb in range(blocks_here):
                        part = scores[kb * BLOCK_TOKENS : (kb + 1) * BLOCK_TOKENS]
                        if own:
                            key_at = lax.broadcasted_iota(jnp.int32, part.shape, 0)
                            row_at = lax.broadcasted_iota(jnp.int32, part.shape, 1) % BLOCK_TOKENS
                            reach = jnp.where(query_block == kb, 0, BLOCK_TOKENS)
                            part = jnp.where(key_at <= row_at + reach, part, -FAR)
                        parts.append(part)
                    new_peak = None
                    for part, cap in zip(parts, caps):
                        top = jnp.minimum(jnp.max(part, axis=0, keepdims=True), cap)
                        new_peak = top if new_peak is None else jnp.maximum(new_peak, top)
                    if not own:
                        old_peak = peak[query_block, h, :, lanes]
                        new_peak = jnp.maximum(new_peak, old_peak)
                    peak[query_block, h, :, lanes] = new_peak
                    level = new_peak * scale
                    weights = [
                        jnp.exp2(part * scale - jnp.maximum(level, floor))
                        for part, floor in zip(parts, floors)
                    ]
                    added = None
                    for w in weights:
                        s = jnp.sum(w, axis=0, keepdims=True)
                        added = s if added is None else added + s
                    low = jnp.concatenate([w.astype(jnp.bfloat16) for w in weights], axis=0)
                    product = jnp.dot(value_part, low, preferred_element_type=jnp.float32)
                    if own:
                        weight_sum[query_block, h, :, lanes] = added
                        total[query_block, h, :, lanes] = product
                    else:
                        fade = jnp.exp2((old_peak - new_peak) * scale)
                        weight_sum[query_block, h, :, lanes] = (
                            weight_sum[query_block, h, :, lanes] * fade + added
                        )
                        total[query_block, h, :, lanes] = (
                            total[query_block, h, :, lanes] * fade + product
                        )
                return carry

            lax.fori_loop(0, blocks_here, one_query_block, 0)

    for piece in range(2):
        loads[piece].wait()
        send_on(me, piece, a, b)
    loads[2].wait()

    def turn_block(query_block, carry):
        at = pl.ds(pl.multiple_of(query_block * BLOCK_TOKENS, BLOCK_TOKENS), BLOCK_TOKENS)
        for h in range(kv_local):
            for g in range(groups):
                head = h * groups + g
                turned_queries[query_block, h, :, pl.ds(g * BLOCK_TOKENS, BLOCK_TOKENS)] = (
                    jnp.transpose(raw_queries[at, pl.ds(head * HEAD_SIZE, HEAD_SIZE)])
                )
        return carry

    lax.fori_loop(0, blocks_here, turn_block, 0)
    attend(me, True)

    rounds = (major + minor - 1) * minor * 4

    def place_of(turn):
        far, near = turn // (4 * minor), (turn // 4) % minor
        up, along = (turn // 2) % 2, turn % 2
        reach = far - near
        i = a + reach * (1 - 2 * up)
        j = b + near * (1 - 2 * along)
        fits = (reach >= 0) & (i >= 0) & (i < major) & (j >= 0) & (j < minor)
        fits = fits & ((reach > 0) | (up == 0)) & ((near > 0) | (along == 0))
        return fits, i, j

    def one_shard(turn, carry):
        fits, i, j = place_of(turn)

        @pl.when(fits & (far_from(i, j)))
        def _():
            slot = i * minor + j
            for piece in range(2):
                pltpu.make_async_copy(
                    held.at[slot, piece], held.at[slot, piece], recv_sem.at[slot, piece]
                ).wait()
                send_on(slot, piece, i, j)
            attend(slot, False)

        return carry

    def far_from(i, j):
        return (i != a) | (j != b)

    lax.fori_loop(1, rounds, one_shard, 0)

    per_peer = blocks_here // tp_size
    wide = kv_local * width

    def finish(query_block, h, put):
        at = pl.ds(pl.multiple_of(query_block * BLOCK_TOKENS, BLOCK_TOKENS), BLOCK_TOKENS)
        for g in range(groups):
            lanes = pl.ds(g * BLOCK_TOKENS, BLOCK_TOKENS)
            bottom = weight_sum[query_block, h, :, lanes]
            normed = (total[query_block, h, :, lanes] * (1.0 / bottom)).astype(jnp.bfloat16)
            put(h * groups + g, jnp.transpose(normed))
            log_norm[pl.ds(h * groups + g, 1), at] = (
                peak[query_block, h, :, lanes] * factor + jnp.log(bottom)
            )

    swaps = []
    for turn in range(1, tp_size + 1):
        peer = (mine + turn) % tp_size
        for k in range(per_peer):
            query_block = peer * per_peer + k
            out_rows = pl.ds(k * BLOCK_TOKENS, BLOCK_TOKENS)
            for h in range(kv_local):
                if turn < tp_size:

                    def put(head, tile, query_block=query_block):
                        leaving[query_block, :, pl.ds(head * HEAD_SIZE, HEAD_SIZE)] = tile

                else:

                    def put(head, tile, out_rows=out_rows):
                        at = pl.multiple_of(mine * wide + head * HEAD_SIZE, HEAD_SIZE)
                        attended[out_rows, pl.ds(at, HEAD_SIZE)] = tile

                finish(query_block, h, put)
                if turn < tp_size:
                    source = pl.ds(h * width, width)
                    target = pl.ds(pl.multiple_of(mine * wide + h * width, HEAD_SIZE), width)
                    copy = pltpu.make_async_remote_copy(
                        src_ref=leaving.at[query_block, :, source],
                        dst_ref=attended.at[out_rows, target],
                        send_sem=swap_send.at[turn - 1, k, h],
                        recv_sem=swap_recv.at[turn - 1, k, h],
                        device_id={"tp": peer},
                        device_id_type=MESH,
                    )
                    copy.start()
                    swaps.append(copy)

    def settle(turn, carry):
        fits, i, j = place_of(turn)

        @pl.when(fits)
        def _():
            slot = i * minor + j
            for piece in range(2):
                for wanted, copy in onward(slot, piece, i, j):

                    @pl.when(wanted)
                    def _(copy=copy):
                        copy.wait_send()

        return carry

    lax.fori_loop(0, rounds, settle, 0)
    for copy in swaps:
        copy.wait()


def body(tp_size, ctx_size, queries, rotated_key_rows, ordered_value_rows, block_order, live_blocks):
    tok_rows, own_columns = queries.shape
    kv_columns = rotated_key_rows.shape[1]
    kv_local = kv_columns // HEAD_SIZE
    heads_local = own_columns // HEAD_SIZE
    groups = heads_local // kv_local
    blocks_here = tok_rows // BLOCK_TOKENS
    width = groups * BLOCK_TOKENS
    major, minor = grid_of(ctx_size)
    dims = (major, minor, tp_size, kv_local, groups, blocks_here, live_blocks.shape[1])
    per_peer = blocks_here // tp_size
    whole = pl.BlockSpec(memory_space=pltpu.VMEM)
    small = pl.BlockSpec(memory_space=pltpu.SMEM)
    apart = pl.BlockSpec(memory_space=pl.ANY)
    return pl.pallas_call(
        functools.partial(kernel, dims),
        out_shape=(
            jax.ShapeDtypeStruct((tok_rows // tp_size, own_columns * tp_size), jnp.bfloat16),
            jax.ShapeDtypeStruct((heads_local, tok_rows), jnp.float32),
        ),
        in_specs=[apart, apart, apart, small, small],
        out_specs=(whole, whole),
        scratch_shapes=[
            pltpu.VMEM((ctx_size, 2, tok_rows, kv_columns), jnp.bfloat16),
            pltpu.VMEM((tok_rows, own_columns), jnp.bfloat16),
            pltpu.VMEM((blocks_here, kv_local, HEAD_SIZE, width), jnp.bfloat16),
            pltpu.VMEM((blocks_here, kv_local, HEAD_SIZE, width), jnp.float32),
            pltpu.VMEM((blocks_here, kv_local, 1, width), jnp.float32),
            pltpu.VMEM((blocks_here, kv_local, 1, width), jnp.float32),
            pltpu.VMEM((blocks_here, BLOCK_TOKENS, own_columns), jnp.bfloat16),
            pltpu.SMEM((2, blocks_here * blocks_here), jnp.float32),
            pltpu.SemaphoreType.DMA((3,)),
            pltpu.SemaphoreType.DMA((ctx_size, 2, 4)),
            pltpu.SemaphoreType.DMA((ctx_size, 2)),
            pltpu.SemaphoreType.DMA((tp_size - 1, per_peer, kv_local)),
            pltpu.SemaphoreType.DMA((tp_size - 1, per_peer, kv_local)),
        ],
        compiler_params=pltpu.CompilerParams(collective_id=0, has_side_effects=True),
        name="gather_attend",
    )(queries, rotated_key_rows, ordered_value_rows, block_order.reshape(1, -1), live_blocks)


def solution(mesh):
    placed = (
        P(("rep", "ctx"), "tp"),
        P(("rep", "ctx"), "tp"),
        P(("rep", "ctx"), "tp"),
        P("rep"),
        P("rep", None),
    )
    return jax.shard_map(
        functools.partial(body, mesh.shape["tp"], mesh.shape["ctx"]),
        mesh=mesh,
        in_specs=placed,
        out_specs=(P(("rep", "ctx", "tp"), None), P(("rep", "tp"), "ctx")),
        check_vma=False,
    )
```

profile of v0, /device:TPU:0, one launch (start us, length us, event | category | flops | bytes accessed | tf_op | source)
XLA Modules:
  0.0 59.2 jit_solution(6806453633876614964)
XLA Ops:
  0.6 55.6 %gather_attend.1 = (bf16[128,4096]{1,0:T(8,128)(2,1)}, f32[16,256]{1,0:T(8,128)}) custom-call(bf16[256,2048]{1,0:T(8,128)(2,1)} %queries.1, bf16[256,256]{1,0:T(8,128)(2,1)} %keys.1, bf16[256,256]{1,0:T(8,128)(2,1)} %values.1, s32[1,16]{1,0:T(1,128)} %bitcast.1, s32[16,12]{1,0:T(8,128)} %live_blocks.1), custom_call_target="tpu_custom_call" | custom-call | tf_op jit(solution)/shard_map/gather_attend/pallas_call | solution.py:313
  56.2 0.0 copy-start
  56.2 2.3 %copy.9 = bf16[128,4096]{1,0:T(8,128)(2,1)} copy(bf16[128,4096]{1,0:T(8,128)(2,1)} %get-tuple-element.4) | data formatting | bytes 2097152
  58.5 0.0 copy-done
  58.5 0.6 %copy.10 = f32[16,256]{1,0:T(8,128)} copy(f32[16,256]{1,0:T(8,128)S(1)} %copy-done) | data formatting | bytes 32768
Async XLA Ops:
  56.2 2.3 %copy-start = (f32[16,256]{1,0:T(8,128)S(1)}, f32[16,256]{1,0:T(8,128)}, u32[]{:S(2)}) copy-start(f32[16,256]{1,0:T(8,128)} %get-tuple-element.5) | copy-start | bytes 49156
where the time goes:
time: 59.4 us; the launch traced here: 59.2 us
  Pallas kernels  55.6 us (94%)
  local copies, waits for them, and re-layouts  2.9 us (5%)
  between operations  0.65 us (1%)
    pallas_call x1, Pallas kernels, body(): pl.pallas_call(functools.partial(kernel, dims), out_shape=(jax.ShapeDtype...  55.6 us
    unnamed x4, local copies, waits for them, and re-layouts  2.9 us

commit v1 on v0

--- a/solution.py
+++ b/solution.py
@@ -11,6 +11,8 @@
 HEAD_SIZE = 128
 BLOCK_TOKENS = 128
 CHUNK = 256
+STRIP = 16
+SLOTS = 3
 FAR = 1e30
 HUGE = 3e38
 MESH = pl.DeviceIdType.MESH
@@ -38,6 +40,7 @@
     weight_sum,
     leaving,
     limits,
+    scores,
     load_sem,
     send_sem,
     recv_sem,
@@ -121,63 +124,78 @@
 
     def attend(slot, own):
         find_limits(slot)
-        for h in range(kv_local):
-            columns = pl.ds(h * HEAD_SIZE, HEAD_SIZE)
-            key_part = held[slot, 0, :, columns]
-            value_part = jnp.transpose(held[slot, 1, :, columns])
-
-            def one_query_block(query_block, carry):
-                caps = [limits[0, query_block * blocks_here + kb] for kb in range(blocks_here)]
-                floors = [limits[1, query_block * blocks_here + kb] for kb in range(blocks_here)]
-                for start in range(0, width, CHUNK):
-                    lanes = pl.ds(start, CHUNK)
-                    scores = jnp.dot(
-                        key_part,
-                        turned_queries[query_block, h, :, lanes],
-                        preferred_element_type=jnp.float32,
-                    )
-                    parts = []
-                    for kb in range(blocks_here):
-                        part = scores[kb * BLOCK_TOKENS : (kb + 1) * BLOCK_TOKENS]
-                        if own:
-                            key_at = lax.broadcasted_iota(jnp.int32, part.shape, 0)
-                            row_at = lax.broadcasted_iota(jnp.int32, part.shape, 1) % BLOCK_TOKENS
-                            reach = jnp.where(query_block == kb, 0, BLOCK_TOKENS)
-                            part = jnp.where(key_at <= row_at + reach, part, -FAR)
-                        parts.append(part)
-                    new_peak = None
-                    for part, cap in zip(parts, caps):
-                        top = jnp.minimum(jnp.max(part, axis=0, keepdims=True), cap)
-                        new_peak = top if new_peak is None else jnp.maximum(new_peak, top)
-                    if not own:
-                        old_peak = peak[query_block, h, :, lanes]
-                        new_peak = jnp.maximum(new_peak, old_peak)
-                    peak[query_block, h, :, lanes] = new_peak
-                    level = new_peak * scale
-                    weights = [
-                        jnp.exp2(part * scale - jnp.maximum(level, floor))
-                        for part, floor in zip(parts, floors)
-                    ]
-                    added = None
-                    for w in weights:
-                        s = jnp.sum(w, axis=0, keepdims=True)
-                        added = s if added is None else added + s
-                    low = jnp.concatenate([w.astype(jnp.bfloat16) for w in weights], axis=0)
-                    product = jnp.dot(value_part, low, preferred_element_type=jnp.float32)
-                    if own:
-                        weight_sum[query_block, h, :, lanes] = added
-                        total[query_block, h, :, lanes] = product
-                    else:
-                        fade = jnp.exp2((old_peak - new_peak) * scale)
-                        weight_sum[query_block, h, :, lanes] = (
-                            weight_sum[query_block, h, :, lanes] * fade + added
-                        )
-                        total[query_block, h, :, lanes] = (
-                            total[query_block, h, :, lanes] * fade + product
-                        )
-                return carry
-
-            lax.fori_loop(0, blocks_here, one_query_block, 0)
+        keys_here = blocks_here * BLOCK_TOKENS
+        units = [
+            (query_block, h, start)
+            for h in range(kv_local)
+            for query_block in range(blocks_here)
+            for start in range(0, width, CHUNK)
+        ]
+        turned_values = [
+            jnp.transpose(held[slot, 1, :, pl.ds(h * HEAD_SIZE, HEAD_SIZE)])
+            for h in range(kv_local)
+        ]
+
+        def score(u):
+            query_block, h, start = units[u]
+            part = jnp.dot(
+                held[slot, 0, :, pl.ds(h * HEAD_SIZE, HEAD_SIZE)],
+                turned_queries[query_block, h, :, pl.ds(start, CHUNK)],
+                preferred_element_type=jnp.float32,
+            )
+            tops = []
+            for kb in range(blocks_here):
+                block = part[kb * BLOCK_TOKENS : (kb + 1) * BLOCK_TOKENS]
+                if own and kb == query_block:
+                    key_at = lax.broadcasted_iota(jnp.int32, block.shape, 0)
+                    row_at = lax.broadcasted_iota(jnp.int32, block.shape, 1) % BLOCK_TOKENS
+                    block = jnp.where(key_at <= row_at, block, -FAR)
+                scores[u % SLOTS, pl.ds(kb * BLOCK_TOKENS, BLOCK_TOKENS), :] = block
+                tops.append(jnp.max(block, axis=0, keepdims=True))
+            return tops
+
+        def absorb(u, tops):
+            query_block, h, start = units[u]
+            lanes = pl.ds(start, CHUNK)
+            first = query_block * blocks_here
+            new_peak = None
+            for kb, top in enumerate(tops):
+                top = jnp.minimum(top, limits[0, first + kb])
+                new_peak = top if new_peak is None else jnp.maximum(new_peak, top)
+            if not own:
+                old_peak = peak[query_block, h, :, lanes]
+                new_peak = jnp.maximum(new_peak, old_peak)
+            peak[query_block, h, :, lanes] = new_peak
+            level = new_peak * scale
+            added = None
+            low = []
+            for kb in range(blocks_here):
+                floor = jnp.maximum(level, limits[1, first + kb])
+                for at in range(kb * BLOCK_TOKENS, (kb + 1) * BLOCK_TOKENS, STRIP):
+                    w = jnp.exp2(scores[u % SLOTS, pl.ds(at, STRIP), :] * scale - floor)
+                    added = w if added is None else added + w
+                    low.append(w.astype(jnp.bfloat16))
+            added = jnp.sum(added, axis=0, keepdims=True)
+            product = jnp.dot(
+                turned_values[h],
+                jnp.concatenate(low, axis=0),
+                preferred_element_type=jnp.float32,
+            )
+            if own:
+                weight_sum[query_block, h, :, lanes] = added
+                total[query_block, h, :, lanes] = product
+            else:
+                fade = jnp.exp2((old_peak - new_peak) * scale)
+                weight_sum[query_block, h, :, lanes] = (
+                    weight_sum[query_block, h, :, lanes] * fade + added
+                )
+                total[query_block, h, :, lanes] = total[query_block, h, :, lanes] * fade + product
+
+        waiting = [score(u) for u in range(SLOTS - 1)]
+        for u in range(len(units)):
+            if u + SLOTS - 1 < len(units):
+                waiting.append(score(u + SLOTS - 1))
+            absorb(u, waiting[u])
 
     for piece in range(2):
         loads[piece].wait()
@@ -327,6 +345,7 @@
             pltpu.VMEM((blocks_here, kv_local, 1, width), jnp.float32),
             pltpu.VMEM((blocks_here, BLOCK_TOKENS, own_columns), jnp.bfloat16),
             pltpu.SMEM((2, blocks_here * blocks_here), jnp.float32),
+            pltpu.VMEM((SLOTS, tok_rows, CHUNK), jnp.float32),
             pltpu.SemaphoreType.DMA((3,)),
             pltpu.SemaphoreType.DMA((ctx_size, 2, 4)),
             pltpu.SemaphoreType.DMA((ctx_size, 2)),

time: 59.4 us -> 40.7 us (0.69)
  Pallas kernels: 55.6 us -> 36.9 us
    pallas_call x1, Pallas kernels: 55.6 us -> 36.9 us  [body(): pl.pallas_call(functools.partial(kernel, dims), out_shape=(jax.ShapeDtype...]
where the time goes in v1:
time: 40.7 us; the launch traced here: 40.5 us
  Pallas kernels  36.9 us (91%)
  local copies, waits for them, and re-layouts  2.9 us (7%)
  between operations  0.65 us (2%)
    pallas_call x1, Pallas kernels, body(): pl.pallas_call(functools.partial(kernel, dims), out_shape=(jax.ShapeDtype...  36.9 us
    unnamed x4, local copies, waits for them, and re-layouts  2.9 us

profile of v1, /device:TPU:0, one launch (start us, length us, event | category | flops | bytes accessed | tf_op | source)
XLA Modules:
  0.0 40.5 jit_solution(10181626132531551732)
XLA Ops:
  0.6 36.9 %gather_attend.1 = (bf16[128,4096]{1,0:T(8,128)(2,1)}, f32[16,256]{1,0:T(8,128)}) custom-call(bf16[256,2048]{1,0:T(8,128)(2,1)} %queries.1, bf16[256,256]{1,0:T(8,128)(2,1)} %keys.1, bf16[256,256]{1,0:T(8,128)(2,1)} %values.1, s32[1,16]{1,0:T(1,128)} %bitcast.1, s32[16,12]{1,0:T(8,128)} %live_blocks.1), custom_call_target="tpu_custom_call" | custom-call | tf_op jit(solution)/shard_map/gather_attend/pallas_call | solution.py:331
  37.5 0.0 copy-start
  37.6 2.3 %copy.9 = bf16[128,4096]{1,0:T(8,128)(2,1)} copy(bf16[128,4096]{1,0:T(8,128)(2,1)} %get-tuple-element.4) | data formatting | bytes 2097152
  39.8 0.0 copy-done
  39.9 0.6 %copy.10 = f32[16,256]{1,0:T(8,128)} copy(f32[16,256]{1,0:T(8,128)S(1)} %copy-done) | data formatting | bytes 32768
Async XLA Ops:
  37.5 2.3 %copy-start = (f32[16,256]{1,0:T(8,128)S(1)}, f32[16,256]{1,0:T(8,128)}, u32[]{:S(2)}) copy-start(f32[16,256]{1,0:T(8,128)} %get-tuple-element.5) | copy-start | bytes 49156

commit v2 on v1

--- a/solution.py
+++ b/solution.py
@@ -328,11 +328,11 @@
     whole = pl.BlockSpec(memory_space=pltpu.VMEM)
     small = pl.BlockSpec(memory_space=pltpu.SMEM)
     apart = pl.BlockSpec(memory_space=pl.ANY)
-    return pl.pallas_call(
+    results = pl.pallas_call(
         functools.partial(kernel, dims),
         out_shape=(
-            jax.ShapeDtypeStruct((tok_rows // tp_size, own_columns * tp_size), jnp.bfloat16),
-            jax.ShapeDtypeStruct((heads_local, tok_rows), jnp.float32),
+            pltpu.VMEM((tok_rows // tp_size, own_columns * tp_size), jnp.bfloat16),
+            pltpu.VMEM((heads_local, tok_rows), jnp.float32),
         ),
         in_specs=[apart, apart, apart, small, small],
         out_specs=(whole, whole),
@@ -355,6 +355,7 @@
         compiler_params=pltpu.CompilerParams(collective_id=0, has_side_effects=True),
         name="gather_attend",
     )(queries, rotated_key_rows, ordered_value_rows, block_order.reshape(1, -1), live_blocks)
+    return results
 
 
 def solution(mesh):

time: 40.7 us -> 38.4 us (0.943)
  local copies, waits for them, and re-layouts: 2.9 us -> 1.58 us
  Pallas kernels: 36.9 us -> 35.9 us
    unnamed x4 -> x2, local copies, waits for them, and re-layouts: 2.9 us -> 1.58 us
    pallas_call x1, Pallas kernels: 36.9 us -> 35.9 us  [body(): pl.pallas_call(functools.partial(kernel, dims), out_shape=(pltpu.VMEM((to...]
where the time goes in v2:
time: 38.4 us; the launch traced here: 38.1 us
  Pallas kernels  35.9 us (93%)
  local copies, waits for them, and re-layouts  1.58 us (4%)
  between operations  0.64 us (2%)
    pallas_call x1, Pallas kernels, body(): pl.pallas_call(functools.partial(kernel, dims), out_shape=(pltpu.VMEM((to...  35.9 us
    unnamed x2, local copies, waits for them, and re-layouts  1.58 us

profile of v2, /device:TPU:0, one launch (start us, length us, event | category | flops | bytes accessed | tf_op | source)
XLA Modules:
  0.0 38.1 jit_solution(8547923978707520037)
XLA Ops:
  0.6 35.9 %gather_attend.1 = (bf16[128,4096]{1,0:T(8,128)(2,1)S(1)}, f32[16,256]{1,0:T(8,128)S(1)}) custom-call(bf16[256,2048]{1,0:T(8,128)(2,1)} %queries.1, bf16[256,256]{1,0:T(8,128)(2,1)} %keys.1, bf16[256,256]{1,0:T(8,128)(2,1)} %values.1, s32[1,16]{1,0:T(1,128)} %bitcast.1, s32[16,12]{1,0:T(8,128)} %live_blocks.1), custom_call_target="tpu_custom_call" | custom-call | tf_op jit(solution)/shard_map/gather_attend/pallas_call | solution.py:331
  36.6 1.0 %copy.9 = bf16[128,4096]{1,0:T(8,128)(2,1)} copy(bf16[128,4096]{1,0:T(8,128)(2,1)S(1)} %get-tuple-element.2) | data formatting | bytes 2097152
  37.5 0.6 %copy.10 = f32[16,256]{1,0:T(8,128)} copy(f32[16,256]{1,0:T(8,128)S(1)} %get-tuple-element.3) | data formatting | bytes 32768

commit v3 on v2

--- a/solution.py
+++ b/solution.py
@@ -12,7 +12,7 @@
 BLOCK_TOKENS = 128
 CHUNK = 256
 STRIP = 16
-SLOTS = 3
+SLOTS = 4
 FAR = 1e30
 HUGE = 3e38
 MESH = pl.DeviceIdType.MESH

time: 38.4 us -> 36.3 us (0.945)
  the two profiles are of different devices: /device:TPU:0 before, /device:TPU:26 now
where the time goes in v3:
time: 36.3 us; the launch traced here: 36.1 us
  Pallas kernels  33.9 us (93%)
  local copies, waits for them, and re-layouts  1.58 us (4%)
  between operations  0.64 us (2%)
    pallas_call x1, Pallas kernels, body(): pl.pallas_call(functools.partial(kernel, dims), out_shape=(pltpu.VMEM((to...  33.9 us
    unnamed x2, local copies, waits for them, and re-layouts  1.58 us

profile of v3, /device:TPU:26, one launch (start us, length us, event | category | flops | bytes accessed | tf_op | source)
XLA Modules:
  0.0 36.1 jit_solution(2187846530234544280)
XLA Ops:
  0.6 33.9 %gather_attend.1 = (bf16[128,4096]{1,0:T(8,128)(2,1)S(1)}, f32[16,256]{1,0:T(8,128)S(1)}) custom-call(bf16[256,2048]{1,0:T(8,128)(2,1)} %queries.1, bf16[256,256]{1,0:T(8,128)(2,1)} %keys.1, bf16[256,256]{1,0:T(8,128)(2,1)} %values.1, s32[1,16]{1,0:T(1,128)} %bitcast.1, s32[16,12]{1,0:T(8,128)} %live_blocks.1), custom_call_target="tpu_custom_call" | custom-call | tf_op jit(solution)/shard_map/gather_attend/pallas_call | solution.py:331
  34.5 1.0 %copy.9 = bf16[128,4096]{1,0:T(8,128)(2,1)} copy(bf16[128,4096]{1,0:T(8,128)(2,1)S(1)} %get-tuple-element.2) | data formatting | bytes 2097152
  35.5 0.6 %copy.10 = f32[16,256]{1,0:T(8,128)} copy(f32[16,256]{1,0:T(8,128)S(1)} %get-tuple-element.3) | data formatting | bytes 32768
